TPU v7x, 32 devices: a whole 2x2x4 slice. The times are simulated.
32 devices in a mesh: inter: 16 (over z, y, x), intra: 2 (over core).
Axes of the slice: x: 2, y: 2, z: 4, core: 2. Of those that a mesh axis runs over, the one named last changes fastest.
Arguments:
- tokens: bfloat16 [2048, 4096], P('inter', 'intra'), may hold values from -6 to 6
- gate_codes: bfloat16 [7168, 4096], P(('intra', 'inter')), may hold values from -127 to 127
- gate_scales: float32 [7168, 16], P(('intra', 'inter')), may hold values from 0.0001 to 0.0005
- up_codes: bfloat16 [7168, 4096], P(('intra', 'inter')), may hold values from -127 to 127
- up_scales: float32 [7168, 16], P(('intra', 'inter')), may hold values from 0.0001 to 0.0005
- cotangent: bfloat16 [2048, 7168], P('inter', 'intra'), may hold values from -6 to 6
Outputs:
- hidden: bfloat16 [2048, 7168], P('inter', 'intra')
- token_grad: bfloat16 [2048, 4096], P('inter', 'intra')
- gate_grad: float32 [7168, 4096], P(('intra', 'inter'))
- up_grad: float32 [7168, 4096], P(('intra', 'inter'))
All inputs are finite; a program needn't handle non-finite values.
Results may differ from a plain program's by a relative error of at most 0.02.
Values may be sent and summed in bfloat16 or wider, within the bound.
A program may use at most 384 MiB of HBM per device.

v0:
```python
import jax
import jax.numpy as jnp
from jax import lax
from jax.sharding import PartitionSpec as P


def dequantize(codes, scales):
    rows, width = codes.shape
    blocks = scales.shape[1]
    step = width // blocks
    parts = [
        codes[:, b * step : (b + 1) * step].astype(jnp.float32) * scales[:, b : b + 1]
        for b in range(blocks)
    ]
    return jnp.concatenate(parts, axis=1).astype(jnp.bfloat16)


def per_device(tokens, gate_codes, gate_scales, up_codes, up_scales, cotangent):
    groups = lax.axis_size("inter")
    mine = lax.all_gather(tokens, "inter", axis=0, tiled=True)
    whole = lax.all_gather(mine, "intra", axis=0, tiled=False)
    slabs, count, wide = whole.shape
    back = lax.all_to_all(cotangent, "inter", split_axis=1, concat_axis=0, tiled=True)
    w_gate = dequantize(gate_codes, gate_scales)
    w_up = dequantize(up_codes, up_scales)

    def forward(weights):
        total = None
        for s in range(slabs):
            term = lax.dot_general(
                whole[s],
                weights[:, s * wide : (s + 1) * wide],
                (((1,), (1,)), ((), ())),
                preferred_element_type=jnp.float32,
            )
            total = term if total is None else total + term
        return total

    gate = forward(w_gate)
    up = forward(w_up)
    sig = jax.nn.sigmoid(gate)
    act = gate * sig
    hidden = (act * up).astype(jnp.bfloat16)
    back = back.astype(jnp.float32)
    d_up = (back * act).astype(jnp.bfloat16)
    d_gate = (back * up * sig * (1.0 + gate * (1.0 - sig))).astype(jnp.bfloat16)
    hidden = lax.all_to_all(hidden, "inter", split_axis=0, concat_axis=1, tiled=True)
    partial_sum = jnp.dot(d_gate, w_gate, preferred_element_type=jnp.float32)
    partial_sum = partial_sum + jnp.dot(d_up, w_up, preferred_element_type=jnp.float32)
    partial_sum = lax.psum_scatter(
        partial_sum.astype(jnp.bfloat16), "intra", scatter_dimension=1, tiled=True
    )
    token_grad = lax.psum_scatter(partial_sum, "inter", scatter_dimension=0, tiled=True)

    def rows_grad(d_rows):
        terms = [
            lax.dot_general(
                d_rows, whole[s], (((0,), (0,)), ((), ())), preferred_element_type=jnp.float32
            )
            for s in range(slabs)
        ]
        return jnp.concatenate(terms, axis=1) / groups

    return (hidden, token_grad, rows_grad(d_gate), rows_grad(d_up))


def solution(mesh):
    return jax.shard_map(
        per_device,
        mesh=mesh,
        in_specs=(
            P("inter", "intra"),
            P(("intra", "inter"), None),
            P(("intra", "inter"), None),
            P(("intra", "inter"), None),
            P(("intra", "inter"), None),
            P("inter", "intra"),
        ),
        out_specs=(
            P("inter", "intra"),
            P("inter", "intra"),
            P(("intra", "inter"), None),
            P(("intra", "inter"), None),
        ),
        check_vma=False,
    )
```

profile of v0, /device:TPU:26, one launch (start us, length us, event | category | flops | bytes accessed | tf_op | source)
XLA Modules:
  0.0 465.3 jit_solution(1570176110932852104)
XLA Ops:
  7.9 114.0 %all-gather.4.cloned.1.call-done = bf16[2048,2048]{1,0:T(8,128)(2,1)} async-done(((bf16[128,2048]{1,0:T(8,128)(2,1)}), bf16[2048,2048]{1,0:T(8,128)(2,1)}) %all-gather.4.cloned.1.call-update) | async-done | bytes 8388624 | tf_op jit(solution)/shard_map/all_gather | solution.py:20
  124.4 6.3 %all-to-all-start.1 = ((bf16[128,16,224]{0,2,1:T(8,128)(2,1)}), bf16[128,16,224]{0,2,1:T(8,128)(2,1)S(1)}, u32[]{:S(2)}, u32[]{:S(2)}) async-start(bf16[128,16,224]{0,2,1:T(8,128)(2,1)} %bitcast.36), calls=%async_computation.1 | async-start | bytes 1835008 | tf_op jit(solution)/shard_map/all_to_all | solution.py:23
  141.2 1.7 constant_dynamic-update-slice_fusion.47
  143.0 1.7 constant_dynamic-update-slice_fusion.46
  144.7 1.7 constant_dynamic-update-slice_fusion.45
  154.6 1.8 constant_dynamic-update-slice_fusion.39
  164.3 1.7 constant_dynamic-update-slice_fusion.38
  166.0 1.7 constant_dynamic-update-slice_fusion.37
  169.4 1.7 constant_dynamic-update-slice_fusion.35
  176.1 7.7 %fusion.2 = f32[224,2048]{1,0:T(8,128)} fusion(bf16[224,2048]{1,0:T(8,128)(2,1)} %copy-done.7, bf16[4096,2048]{1,0:T(8,128)(2,1)} %all-gather.6.cloned.1.call-done), kind=kOutput, calls=%fused_computation.3 | convolution fusion | flops 1879048192 | bytes 11141120 | tf_op jit(solution)/shard_map/dot_general | solution.py:30
  183.8 6.7 %fusion.4 = f32[224,2048]{1,0:T(8,128)S(1)} fusion(bf16[224,2048]{1,0:T(8,128)(2,1)} %get-tuple-element.44, bf16[4096,2048]{1,0:T(8,128)(2,1)} %all-gather.6.cloned.1.call-done), kind=kOutput, calls=%fused_computation.5 | convolution fusion | flops 1879048192 | bytes 11141120 | tf_op jit(solution)/shard_map/dot_general | solution.py:30
  190.5 3.9 fusion.19
  195.3 9.3 %fusion.31 = (bf16[2048,224]{0,1:T(8,128)(2,1)S(1)}, bf16[2048,224]{0,1:T(8,128)(2,1)S(1)}, bf16[28,16,8,128]{3,2,1,0:T(8,128)(2,1)}) fusion(f32[2048,224]{0,1:T(8,128)} %fusion.19, f32[224,2048]{1,0:T(8,128)} %fusion.2, bf16[224,2048]{1,0:T(8,128)(2,1)} %copy-done.8, bf16[4096,2048]{1,0:T(8,128)(2,1)} %all-gather.6.cloned.1.call-done, ...), kind=kOutput, calls=%fused_computation.28 | convolution fusion | flops 1886846976 | bytes 16646144 | tf_op jit(solution)/shard_map/dot_general | solution.py:30
  204.6 15.0 %fusion.38 = f32[2048,4096]{1,0:T(8,128)} fusion(bf16[2048,224]{0,1:T(8,128)(2,1)S(1)} %get-tuple-element.9, bf16[224,4096]{1,0:T(8,128)(2,1)} %get-tuple-element.43), kind=kOutput, calls=%fused_computation.133 | convolution fusion | flops 3758096384 | bytes 36306944 | tf_op jit(solution)/shard_map/dot_general | solution.py:48
  219.6 16.9 %add_convert_fusion = bf16[2048,4096]{1,0:T(8,128)(2,1)} fusion(f32[2048,4096]{1,0:T(8,128)} %fusion.38, bf16[2048,224]{0,1:T(8,128)(2,1)S(1)} %get-tuple-element.8, bf16[224,4096]{1,0:T(8,128)(2,1)S(1)} %get-tuple-element.11), kind=kOutput, calls=%fused_computation | convolution fusion | flops 3774873600 | bytes 53084160 | tf_op jit(solution)/shard_map/dot_general | solution.py:49
  236.6 26.3 %reduce-scatter.3.cloned.1.call-done = bf16[2048,2048]{1,0:T(8,128)(2,1)} async-done(((bf16[2048,4096]{1,0:T(8,128)(2,1)}), bf16[2048,2048]{1,0:T(8,128)(2,1)}) %reduce-scatter.3.cloned.1.call-update) | async-done | bytes 8388624 | tf_op jit(solution)/shard_map/reduce_scatter | solution.py:50
  265.1 6.9 %all-to-all-start = ((bf16[16,128,224]{1,2,0:T(8,128)(2,1)}), bf16[16,128,224]{1,2,0:T(8,128)(2,1)S(1)}, u32[]{:S(2)}, u32[]{:S(2)}) async-start(bf16[16,128,224]{1,2,0:T(8,128)(2,1)} %bitcast.73), calls=%async_computation | async-start | bytes 1835008 | tf_op jit(solution)/shard_map/all_to_all | solution.py:47
  272.1 5.9 %fusion.6 = f32[224,2048]{1,0:T(8,128)S(1)} fusion(bf16[2048,224]{0,1:T(8,128)(2,1)S(1)} %copy-done.4, bf16[4096,2048]{1,0:T(8,128)(2,1)} %all-gather.6.cloned.1.call-done), kind=kOutput, calls=%fused_computation.7 | convolution fusion | flops 1879048192 | bytes 11141120 | tf_op jit(solution)/shard_map/dot_general | solution.py:57
  278.0 5.6 %fusion.14 = f32[224,2048]{1,0:T(8,128)S(1)} fusion(bf16[2048,224]{0,1:T(8,128)(2,1)S(1)} %copy-done.4, bf16[4096,2048]{1,0:T(8,128)(2,1)} %all-gather.6.cloned.1.call-done), kind=kOutput, calls=%fused_computation.15 | convolution fusion | flops 1879048192 | bytes 11141120 | tf_op jit(solution)/shard_map/dot_general | solution.py:57
  283.8 2.1 fusion
  285.9 2.1 fusion.8
  288.1 3.5 maximum_multiply_fusion
  291.6 14.6 %all-to-all-done = bf16[16,128,224]{1,2,0:T(8,128)(2,1)S(1)} async-done(((bf16[16,128,224]{1,2,0:T(8,128)(2,1)}), bf16[16,128,224]{1,2,0:T(8,128)(2,1)S(1)}, u32[]{:S(2)}, u32[]{:S(2)}) %all-to-all-start) | async-done | bytes 917536 | tf_op jit(solution)/shard_map/all_to_all | solution.py:47
  307.5 151.2 %reduce-scatter.5.cloned.1.call-done = bf16[128,2048]{1,0:T(8,128)(2,1)} async-done(((bf16[2048,2048]{1,0:T(8,128)(2,1)}), bf16[128,2048]{1,0:T(8,128)(2,1)}) %reduce-scatter.5.cloned.1.call-update) | async-done | bytes 524304 | tf_op jit(solution)/shard_map/reduce_scatter | solution.py:53
  (73 shorter events, 41.2 us)
Async XLA Ops:
  7.2 114.8 %all-gather.4.cloned.1.call-start = ((), (), s32[]{:S(2)}) async-start(), calls=%async_computation.4 | async-start | bytes 8912896 | tf_op jit(solution)/shard_map/all_gather | solution.py:20
  7.9 168.2 %all-gather.6.cloned.1.call-start = ((), (), s32[]{:S(2)}) async-start(), calls=%async_computation.7 | async-start | bytes 25165824 | tf_op jit(solution)/shard_map/all_gather | solution.py:21
  122.0 1.2 copy-start
  123.1 7.6 %copy-start.5 = (f32[224,16]{0,1:T(8,128)S(1)}, f32[224,16]{0,1:T(8,128)}, u32[]{:S(2)}) copy-start(f32[224,16]{0,1:T(8,128)} %param.8) | copy-start | bytes 43012
  123.1 7.6 %copy-start.6 = (f32[224,16]{0,1:T(8,128)S(1)}, f32[224,16]{0,1:T(8,128)}, u32[]{:S(2)}) copy-start(f32[224,16]{0,1:T(8,128)} %param.10) | copy-start | bytes 43012
  124.4 70.0 %all-to-all-start.1 = ((bf16[128,16,224]{0,2,1:T(8,128)(2,1)}), bf16[128,16,224]{0,2,1:T(8,128)(2,1)S(1)}, u32[]{:S(2)}, u32[]{:S(2)}) async-start(bf16[128,16,224]{0,2,1:T(8,128)(2,1)} %bitcast.36), calls=%async_computation.1 | async-start | bytes 1835008 | tf_op jit(solution)/shard_map/all_to_all | solution.py:23
  130.7 132.2 %reduce-scatter.3.cloned.1.call-start = ((), (), s32[]{:S(2)}) async-start(), calls=%async_computation.5 | async-start | bytes 25165824 | tf_op jit(solution)/shard_map/reduce_scatter | solution.py:50
  139.2 1.0 copy-start.8
  154.6 14.8 %copy-start.9 = (bf16[224,2048]{1,0:T(8,128)(2,1)}, bf16[224,2048]{1,0:T(8,128)(2,1)S(1)}, u32[]{:S(2)}) copy-start(bf16[224,2048]{1,0:T(8,128)(2,1)S(1)} %get-tuple-element.60) | copy-start | bytes 2752516
  163.4 0.9 copy-start.7
  176.1 14.4 %copy-start.11 = (bf16[4096,2048]{1,0:T(8,128)(2,1)S(1)}, bf16[4096,2048]{1,0:T(8,128)(2,1)}, u32[]{:S(2)}) copy-start(bf16[4096,2048]{1,0:T(8,128)(2,1)} %all-gather.6.cloned.1.call-done) | copy-start | bytes 50331652
  183.8 6.7 %copy-start.10 = (bf16[224,2048]{1,0:T(8,128)(2,1)S(1)}, bf16[224,2048]{1,0:T(8,128)(2,1)}, u32[]{:S(2)}) copy-start(bf16[224,2048]{1,0:T(8,128)(2,1)} %copy-done.9) | copy-start | bytes 2752516
  194.4 0.9 copy-start.1
  204.6 15.0 %copy-start.3 = (bf16[2048,224]{0,1:T(8,128)(2,1)}, bf16[2048,224]{0,1:T(8,128)(2,1)S(1)}, u32[]{:S(2)}) copy-start(bf16[2048,224]{0,1:T(8,128)(2,1)S(1)} %get-tuple-element.8) | copy-start | bytes 2752516
  236.5 222.2 %reduce-scatter.5.cloned.1.call-start = ((), (), s32[]{:S(2)}) async-start(), calls=%async_computation.6 | async-start | bytes 8912896 | tf_op jit(solution)/shard_map/reduce_scatter | solution.py:53
  262.9 1.2 copy-start.2
  264.0 8.0 %copy-start.4 = (bf16[2048,224]{0,1:T(8,128)(2,1)S(1)}, bf16[2048,224]{0,1:T(8,128)(2,1)}, u32[]{:S(2)}) copy-start(bf16[2048,224]{0,1:T(8,128)(2,1)} %copy-done.3) | copy-start | bytes 2752516
  265.1 41.1 %all-to-all-start = ((bf16[16,128,224]{1,2,0:T(8,128)(2,1)}), bf16[16,128,224]{1,2,0:T(8,128)(2,1)S(1)}, u32[]{:S(2)}, u32[]{:S(2)}) async-start(bf16[16,128,224]{1,2,0:T(8,128)(2,1)} %bitcast.73), calls=%async_computation | async-start | bytes 1835008 | tf_op jit(solution)/shard_map/all_to_all | solution.py:47
  272.1 11.5 %slice-start = ((s8[16777216]{0:T(1024)(128)(4,1)}), s8[4194304]{0:T(1024)(128)(4,1)S(1)}, s32[]{:S(2)}) async-start(s8[16777216]{0:T(1024)(128)(4,1)} %bitcast.107), calls=%async_computation.8 | async-start | bytes 8388608
  272.1 11.5 %slice-start.1 = ((s8[16777216]{0:T(1024)(128)(4,1)}), s8[4194304]{0:T(1024)(128)(4,1)S(1)}, s32[]{:S(2)}) async-start(s8[16777216]{0:T(1024)(128)(4,1)} %bitcast.107), calls=%async_computation.9 | async-start | bytes 8388608
  277.9 5.6 %slice-start.2 = ((s8[16777216]{0:T(1024)(128)(4,1)}), s8[4194304]{0:T(1024)(128)(4,1)S(1)}, s32[]{:S(2)}) async-start(s8[16777216]{0:T(1024)(128)(4,1)} %bitcast.107), calls=%async_computation.10 | async-start | bytes 8388608
  278.0 5.8 %slice-start.3 = ((s8[16777216]{0:T(1024)(128)(4,1)}), s8[4194304]{0:T(1024)(128)(4,1)S(1)}, s32[]{:S(2)}) async-start(s8[16777216]{0:T(1024)(128)(4,1)} %bitcast.107), calls=%async_computation.11 | async-start | bytes 8388608
Sparse Core Ops, SparseCore 0:
  10.7 111.1 all-gather.3
  123.5 30.5 all-gather.5
  236.6 26.1 reduce-scatter.2
  265.6 193.1 reduce-scatter.4
where the time goes:
time: 467 us; the launch traced here: 465 us
  waiting for transfers between devices  307 us (66%)
  matrix products  75.2 us (16%)
  other arithmetic  46.8 us (10%)
  between operations  14.1 us (3%)
  starting transfers between devices  13.3 us (3%)
  local copies, waits for them, and re-layouts  8.98 us (2%)
    reduce_scatter x1, waiting for transfers between devices, per_device(): lax.psum_scatter(partial_sum, 'inter', scatter_dimension=0, tiled=True)  151 us
    all_gather x1, waiting for transfers between devices, per_device(): mine = lax.all_gather(tokens, 'inter', axis=0, tiled=True)  114 us
    unnamed x31, other arithmetic  40.6 us
    dot_general x4, matrix products, forward(): lax.dot_general(whole[s], weights[:, s * wide:(s + 1) * wide], (((1,), (1...  27.5 us
    reduce_scatter x1, waiting for transfers between devices, per_device(): lax.psum_scatter(partial_sum.astype(jnp.bfloat16), 'intra', scatter_dimen...  26.3 us
    dot_general x1, matrix products, per_device(): jnp.dot(d_up, w_up, preferred_element_type=jnp.float32)  16.9 us
    dot_general x4, matrix products, rows_grad(): lax.dot_general(d_rows, whole[s], (((0,), (0,)), ((), ())), preferred_ele...  15.7 us
    dot_general x1, matrix products, per_device(): partial_sum = jnp.dot(d_gate, w_gate, preferred_element_type=jnp.float32)  15 us
  transfers between devices with their start and end apart: 6, of which 4 were waited for; matrix products, arithmetic and copies ran while one was open for 18% of the time, Pallas kernels for 0%

commit v1 on v0

--- a/solution.py
+++ b/solution.py
@@ -17,7 +17,13 @@
 
 def per_device(tokens, gate_codes, gate_scales, up_codes, up_scales, cotangent):
     groups = lax.axis_size("inter")
-    mine = lax.all_gather(tokens, "inter", axis=0, tiled=True)
+    x = tokens
+    ways, here, k = (lax.axis_size("inter"), lax.axis_index("inter"), x.shape[0])
+    shape = [n * ways if d == 0 else n for d, n in enumerate(x.shape)]
+    mine = lax.dynamic_update_slice_in_dim(jnp.zeros(shape, x.dtype), x, here * k, axis=0)
+    for far in range(1, ways):
+        x = lax.ppermute(x, "inter", [(d, (d + 1) % ways) for d in range(ways)])
+        mine = lax.dynamic_update_slice_in_dim(mine, x, (here - far) % ways * k, axis=0)
     whole = lax.all_gather(mine, "intra", axis=0, tiled=False)
     slabs, count, wide = whole.shape
     back = lax.all_to_all(cotangent, "inter", split_axis=1, concat_axis=0, tiled=True)

time: 467 us -> 583 us (1.25)
  starting transfers between devices: 13.3 us -> 92.4 us
  waiting for transfers between devices: 307 us -> 327 us
  local copies, waits for them, and re-layouts: 8.98 us -> 28.9 us
    ppermute x0 -> x15, waiting for transfers between devices: none -> 136 us  [per_device(): x = lax.ppermute(x, 'inter', [(d, (d + 1) % ways) for d in range(ways)])]
    all_gather x1 -> x0, waiting for transfers between devices: 114 us -> none  [per_device(): mine = lax.all_gather(tokens, 'inter', axis=0, tiled=True)]
    ppermute x0 -> x15, starting transfers between devices: none -> 64.4 us  [per_device(): x = lax.ppermute(x, 'inter', [(d, (d + 1) % ways) for d in range(ways)])]
    all_to_all x1, starting transfers between devices: 6.25 us -> 20.8 us  [per_device(): lax.all_to_all(cotangent, 'inter', split_axis=1, concat_axis=0, tiled=True)]
    dynamic_update_slice x0 -> x16, local copies, waits for them, and re-layouts: none -> 13.5 us  [the longest x15 12.6 us: per_device(): lax.dynamic_update_slice_in_dim(mine, x, (here - far) % ways * k, axis=0)]
  transfers between devices with their start and end apart: 6 -> 20, of which waited for: 4 -> 18; matrix products, arithmetic and copies ran while one was open for 18% -> 16% of each run, Pallas kernels for 0% -> 0%
where the time goes in v1:
time: 583 us; the launch traced here: 581 us
  waiting for transfers between devices  327 us (56%)
  starting transfers between devices  92.4 us (16%)
  matrix products  72.6 us (12%)
  other arithmetic  46.7 us (8%)
  local copies, waits for them, and re-layouts  28.9 us (5%)
  between operations  14.1 us (2%)
    reduce_scatter x1, waiting for transfers between devices, per_device(): lax.psum_scatter(partial_sum, 'inter', scatter_dimension=0, tiled=True)  149 us
    ppermute x15, waiting for transfers between devices, per_device(): x = lax.ppermute(x, 'inter', [(d, (d + 1) % ways) for d in range(ways)])  136 us
    ppermute x15, starting transfers between devices, per_device(): x = lax.ppermute(x, 'inter', [(d, (d + 1) % ways) for d in range(ways)])  64.4 us
    unnamed x31, other arithmetic  40.4 us
    reduce_scatter x1, waiting for transfers between devices, per_device(): lax.psum_scatter(partial_sum.astype(jnp.bfloat16), 'intra', scatter_dimen...  26.3 us
    dot_general x4, matrix products, forward(): lax.dot_general(whole[s], weights[:, s * wide:(s + 1) * wide], (((1,), (1...  24.9 us
    all_to_all x1, starting transfers between devices, per_device(): lax.all_to_all(cotangent, 'inter', split_axis=1, concat_axis=0, tiled=True)  20.8 us
    dot_general x1, matrix products, per_device(): jnp.dot(d_up, w_up, preferred_element_type=jnp.float32)  16.9 us
  transfers between devices with their start and end apart: 20, of which 18 were waited for; matrix products, arithmetic and copies ran while one was open for 16% of the time, Pallas kernels for 0%

profile of v1, /device:TPU:26, one launch (start us, length us, event | category | flops | bytes accessed | tf_op | source)
XLA Modules:
  0.0 581.4 jit_solution(12604652621069001256)
XLA Ops:
  8.8 12.4 %collective-permute-done = bf16[128,2048]{1,0:T(8,128)(2,1)S(1)} collective-permute-done((bf16[128,2048]{1,0:T(8,128)(2,1)}, bf16[128,2048]{1,0:T(8,128)(2,1)S(1)}, u32[]{:S(2)}, u32[]{:S(2)}) %collective-permute-start) | collective-permute-done | bytes 524320 | tf_op jit(solution)/shard_map/ppermute | solution.py:25
  23.5 11.0 %collective-permute-done.1 = bf16[128,2048]{1,0:T(8,128)(2,1)S(1)} collective-permute-done((bf16[128,2048]{1,0:T(8,128)(2,1)S(1)}, bf16[128,2048]{1,0:T(8,128)(2,1)S(1)}, u32[]{:S(2)}, u32[]{:S(2)}) %collective-permute-start.1) | collective-permute-done | bytes 524320 | tf_op jit(solution)/shard_map/ppermute | solution.py:25
  37.2 11.0 %collective-permute-done.2 = bf16[128,2048]{1,0:T(8,128)(2,1)S(1)} collective-permute-done((bf16[128,2048]{1,0:T(8,128)(2,1)S(1)}, bf16[128,2048]{1,0:T(8,128)(2,1)S(1)}, u32[]{:S(2)}, u32[]{:S(2)}) %collective-permute-start.2) | collective-permute-done | bytes 524320 | tf_op jit(solution)/shard_map/ppermute | solution.py:25
  50.1 11.1 %collective-permute-done.3 = bf16[128,2048]{1,0:T(8,128)(2,1)S(1)} collective-permute-done((bf16[128,2048]{1,0:T(8,128)(2,1)S(1)}, bf16[128,2048]{1,0:T(8,128)(2,1)S(1)}, u32[]{:S(2)}, u32[]{:S(2)}) %collective-permute-start.3) | collective-permute-done | bytes 524320 | tf_op jit(solution)/shard_map/ppermute | solution.py:25
  63.3 9.9 %collective-permute-done.4 = bf16[128,2048]{1,0:T(8,128)(2,1)S(1)} collective-permute-done((bf16[128,2048]{1,0:T(8,128)(2,1)S(1)}, bf16[128,2048]{1,0:T(8,128)(2,1)S(1)}, u32[]{:S(2)}, u32[]{:S(2)}) %collective-permute-start.4) | collective-permute-done | bytes 524320 | tf_op jit(solution)/shard_map/ppermute | solution.py:25
  77.5 7.9 %collective-permute-done.5 = bf16[128,2048]{1,0:T(8,128)(2,1)S(1)} collective-permute-done((bf16[128,2048]{1,0:T(8,128)(2,1)S(1)}, bf16[128,2048]{1,0:T(8,128)(2,1)S(1)}, u32[]{:S(2)}, u32[]{:S(2)}) %collective-permute-start.5) | collective-permute-done | bytes 524320 | tf_op jit(solution)/shard_map/ppermute | solution.py:25
  90.7 7.1 %collective-permute-done.6 = bf16[128,2048]{1,0:T(8,128)(2,1)S(1)} collective-permute-done((bf16[128,2048]{1,0:T(8,128)(2,1)S(1)}, bf16[128,2048]{1,0:T(8,128)(2,1)S(1)}, u32[]{:S(2)}, u32[]{:S(2)}) %collective-permute-start.6) | collective-permute-done | bytes 524320 | tf_op jit(solution)/shard_map/ppermute | solution.py:25
  118.8 8.6 %collective-permute-done.8 = bf16[128,2048]{1,0:T(8,128)(2,1)S(1)} collective-permute-done((bf16[128,2048]{1,0:T(8,128)(2,1)S(1)}, bf16[128,2048]{1,0:T(8,128)(2,1)S(1)}, u32[]{:S(2)}, u32[]{:S(2)}) %collective-permute-start.8) | collective-permute-done | bytes 524320 | tf_op jit(solution)/shard_map/ppermute | solution.py:25
  133.8 10.0 %collective-permute-done.9 = bf16[128,2048]{1,0:T(8,128)(2,1)S(1)} collective-permute-done((bf16[128,2048]{1,0:T(8,128)(2,1)S(1)}, bf16[128,2048]{1,0:T(8,128)(2,1)S(1)}, u32[]{:S(2)}, u32[]{:S(2)}) %collective-permute-start.9) | collective-permute-done | bytes 524320 | tf_op jit(solution)/shard_map/ppermute | solution.py:25
  150.0 10.1 %collective-permute-done.10 = bf16[128,2048]{1,0:T(8,128)(2,1)S(1)} collective-permute-done((bf16[128,2048]{1,0:T(8,128)(2,1)S(1)}, bf16[128,2048]{1,0:T(8,128)(2,1)S(1)}, u32[]{:S(2)}, u32[]{:S(2)}) %collective-permute-start.10) | collective-permute-done | bytes 524320 | tf_op jit(solution)/shard_map/ppermute | solution.py:25
  167.3 10.2 %collective-permute-done.11 = bf16[128,2048]{1,0:T(8,128)(2,1)S(1)} collective-permute-done((bf16[128,2048]{1,0:T(8,128)(2,1)S(1)}, bf16[128,2048]{1,0:T(8,128)(2,1)S(1)}, u32[]{:S(2)}, u32[]{:S(2)}) %collective-permute-start.11) | collective-permute-done | bytes 524320 | tf_op jit(solution)/shard_map/ppermute | solution.py:25
  177.5 6.7 %collective-permute-start.12 = (bf16[128,2048]{1,0:T(8,128)(2,1)S(1)}, bf16[128,2048]{1,0:T(8,128)(2,1)S(1)}, u32[]{:S(2)}, u32[]{:S(2)}) collective-permute-start(bf16[128,2048]{1,0:T(8,128)(2,1)S(1)} %collective-permute-done.11), channel_id=1, source_target_pairs={{0,2},{2,4},{4,6},{6,8},{8,10},{10,12},{12,14},{14,16},{16,18},{18... | collective-permute-start | bytes 1572872 | tf_op jit(solution)/shard_map/ppermute | solution.py:25
  185.8 10.0 %collective-permute-done.12 = bf16[128,2048]{1,0:T(8,128)(2,1)S(1)} collective-permute-done((bf16[128,2048]{1,0:T(8,128)(2,1)S(1)}, bf16[128,2048]{1,0:T(8,128)(2,1)S(1)}, u32[]{:S(2)}, u32[]{:S(2)}) %collective-permute-start.12) | collective-permute-done | bytes 524320 | tf_op jit(solution)/shard_map/ppermute | solution.py:25
  203.4 8.8 %collective-permute-done.13 = bf16[128,2048]{1,0:T(8,128)(2,1)S(1)} collective-permute-done((bf16[128,2048]{1,0:T(8,128)(2,1)S(1)}, bf16[128,2048]{1,0:T(8,128)(2,1)S(1)}, u32[]{:S(2)}, u32[]{:S(2)}) %collective-permute-start.13) | collective-permute-done | bytes 524320 | tf_op jit(solution)/shard_map/ppermute | solution.py:25
  212.2 6.1 %collective-permute-start.14 = (bf16[128,2048]{1,0:T(8,128)(2,1)S(1)}, bf16[128,2048]{1,0:T(8,128)(2,1)S(1)}, u32[]{:S(2)}, u32[]{:S(2)}) collective-permute-start(bf16[128,2048]{1,0:T(8,128)(2,1)S(1)} %collective-permute-done.13), channel_id=1, source_target_pairs={{0,2},{2,4},{4,6},{6,8},{8,10},{10,12},{12,14},{14,16},{16,18},{18... | collective-permute-start | bytes 1572872 | tf_op jit(solution)/shard_map/ppermute | solution.py:25
  228.3 20.8 %all-to-all-start.1 = ((bf16[128,16,224]{0,2,1:T(8,128)(2,1)}), bf16[128,16,224]{0,2,1:T(8,128)(2,1)S(1)}, u32[]{:S(2)}, u32[]{:S(2)}) async-start(bf16[128,16,224]{0,2,1:T(8,128)(2,1)} %bitcast.52), calls=%async_computation.1 | async-start | bytes 1835008 | tf_op jit(solution)/shard_map/all_to_all | solution.py:29
  294.5 6.4 %fusion.6 = f32[2048,224]{0,1:T(8,128)S(1)} fusion(bf16[224,2048]{1,0:T(8,128)(2,1)} %copy-done.12, bf16[2,2048,2048]{2,1,0:T(8,128)(2,1)} %all-gather.2.cloned.1.call-done), kind=kOutput, calls=%fused_computation.9 | convolution fusion | flops 1879048192 | bytes 11141120 | tf_op jit(solution)/shard_map/dot_general | solution.py:36
  312.9 9.5 %fusion.13 = (bf16[2048,224]{0,1:T(8,128)(2,1)S(1)}, bf16[2048,224]{0,1:T(8,128)(2,1)S(1)}, bf16[28,16,8,128]{3,2,1,0:T(8,128)(2,1)}) fusion(f32[2048,224]{0,1:T(8,128)} %fusion.9, f32[2048,224]{0,1:T(8,128)} %fusion.7, bf16[224,2048]{1,0:T(8,128)(2,1)} %copy-done.15, bf16[2,2048,2048]{2,1,0:T(8,128)(2,1)} %all-gather.2.cloned.1.call-done, ...), kind=kOutput, calls=%fused_computation.20 | convolution fusion | flops 1886846976 | bytes 16646144 | tf_op jit(solution)/shard_map/dot_general | solution.py:36
  322.4 15.0 %fusion.18 = f32[2048,4096]{1,0:T(8,128)} fusion(bf16[2048,224]{0,1:T(8,128)(2,1)S(1)} %get-tuple-element.13, bf16[224,4096]{1,0:T(8,128)(2,1)} %get-tuple-element.47), kind=kOutput, calls=%fused_computation.141 | convolution fusion | flops 3758096384 | bytes 36306944 | tf_op jit(solution)/shard_map/dot_general | solution.py:54
  337.4 16.9 %add_convert_fusion = bf16[2048,4096]{1,0:T(8,128)(2,1)} fusion(f32[2048,4096]{1,0:T(8,128)} %fusion.18, bf16[2048,224]{0,1:T(8,128)(2,1)S(1)} %get-tuple-element.12, bf16[224,4096]{1,0:T(8,128)(2,1)S(1)} %get-tuple-element.15), kind=kOutput, calls=%fused_computation | convolution fusion | flops 3774873600 | bytes 53084160 | tf_op jit(solution)/shard_map/dot_general | solution.py:55
  354.5 26.3 %reduce-scatter.3.cloned.1.call-done = bf16[2048,2048]{1,0:T(8,128)(2,1)} async-done(((bf16[2048,4096]{1,0:T(8,128)(2,1)}), bf16[2048,2048]{1,0:T(8,128)(2,1)}) %reduce-scatter.3.cloned.1.call-update) | async-done | bytes 8388624 | tf_op jit(solution)/shard_map/reduce_scatter | solution.py:56
  383.0 6.9 %all-to-all-start = ((bf16[16,128,224]{1,2,0:T(8,128)(2,1)}), bf16[16,128,224]{1,2,0:T(8,128)(2,1)S(1)}, u32[]{:S(2)}, u32[]{:S(2)}) async-start(bf16[16,128,224]{1,2,0:T(8,128)(2,1)} %bitcast.117), calls=%async_computation | async-start | bytes 1835008 | tf_op jit(solution)/shard_map/all_to_all | solution.py:53
  409.6 14.6 %all-to-all-done = bf16[16,128,224]{1,2,0:T(8,128)(2,1)S(1)} async-done(((bf16[16,128,224]{1,2,0:T(8,128)(2,1)}), bf16[16,128,224]{1,2,0:T(8,128)(2,1)S(1)}, u32[]{:S(2)}, u32[]{:S(2)}) %all-to-all-start) | async-done | bytes 917536 | tf_op jit(solution)/shard_map/all_to_all | solution.py:53
  425.5 149.4 %reduce-scatter.5.cloned.1.call-done = bf16[128,2048]{1,0:T(8,128)(2,1)} async-done(((bf16[2048,2048]{1,0:T(8,128)(2,1)}), bf16[128,2048]{1,0:T(8,128)(2,1)}) %reduce-scatter.5.cloned.1.call-update) | async-done | bytes 524304 | tf_op jit(solution)/shard_map/reduce_scatter | solution.py:59
  (127 shorter events, 160.6 us)
Async XLA Ops:
  7.2 287.4 %all-gather.2.cloned.1.call-start = ((), (), s32[]{:S(2)}) async-start(), calls=%async_computation.4 | async-start | bytes 25165824 | tf_op jit(solution)/shard_map/all_gather | solution.py:27
  7.2 13.9 %collective-permute-start = (bf16[128,2048]{1,0:T(8,128)(2,1)}, bf16[128,2048]{1,0:T(8,128)(2,1)S(1)}, u32[]{:S(2)}, u32[]{:S(2)}) collective-permute-start(bf16[128,2048]{1,0:T(8,128)(2,1)} %param.6), channel_id=1, source_target_pairs={{0,2},{2,4},{4,6},{6,8},{8,10},{10,12},{12,14},{14,16},{16,18},{18... | collective-permute-start | bytes 1572872 | tf_op jit(solution)/shard_map/ppermute | solution.py:25
  21.1 13.4 %collective-permute-start.1 = (bf16[128,2048]{1,0:T(8,128)(2,1)S(1)}, bf16[128,2048]{1,0:T(8,128)(2,1)S(1)}, u32[]{:S(2)}, u32[]{:S(2)}) collective-permute-start(bf16[128,2048]{1,0:T(8,128)(2,1)S(1)} %collective-permute-done), channel_id=1, source_target_pairs={{0,2},{2,4},{4,6},{6,8},{8,10},{10,12},{12,14},{14,16},{16,18},{18... | collective-permute-start | bytes 1572872 | tf_op jit(solution)/shard_map/ppermute | solution.py:25
  34.5 13.8 %collective-permute-start.2 = (bf16[128,2048]{1,0:T(8,128)(2,1)S(1)}, bf16[128,2048]{1,0:T(8,128)(2,1)S(1)}, u32[]{:S(2)}, u32[]{:S(2)}) collective-permute-start(bf16[128,2048]{1,0:T(8,128)(2,1)S(1)} %collective-permute-done.1), channel_id=1, source_target_pairs={{0,2},{2,4},{4,6},{6,8},{8,10},{10,12},{12,14},{14,16},{16,18},{18... | collective-permute-start | bytes 1572872 | tf_op jit(solution)/shard_map/ppermute | solution.py:25
  48.3 12.9 %collective-permute-start.3 = (bf16[128,2048]{1,0:T(8,128)(2,1)S(1)}, bf16[128,2048]{1,0:T(8,128)(2,1)S(1)}, u32[]{:S(2)}, u32[]{:S(2)}) collective-permute-start(bf16[128,2048]{1,0:T(8,128)(2,1)S(1)} %collective-permute-done.2), channel_id=1, source_target_pairs={{0,2},{2,4},{4,6},{6,8},{8,10},{10,12},{12,14},{14,16},{16,18},{18... | collective-permute-start | bytes 1572872 | tf_op jit(solution)/shard_map/ppermute | solution.py:25
  61.2 36.6 %copy-start.6 = (bf16[128,2048]{1,0:T(8,128)(2,1)}, bf16[128,2048]{1,0:T(8,128)(2,1)S(1)}, u32[]{:S(2)}) copy-start(bf16[128,2048]{1,0:T(8,128)(2,1)S(1)} %collective-permute-done.3) | copy-start | bytes 1572868
  61.2 12.1 %collective-permute-start.4 = (bf16[128,2048]{1,0:T(8,128)(2,1)S(1)}, bf16[128,2048]{1,0:T(8,128)(2,1)S(1)}, u32[]{:S(2)}, u32[]{:S(2)}) collective-permute-start(bf16[128,2048]{1,0:T(8,128)(2,1)S(1)} %collective-permute-done.3), channel_id=1, source_target_pairs={{0,2},{2,4},{4,6},{6,8},{8,10},{10,12},{12,14},{14,16},{16,18},{18... | collective-permute-start | bytes 1572872 | tf_op jit(solution)/shard_map/ppermute | solution.py:25
  73.3 12.1 %collective-permute-start.5 = (bf16[128,2048]{1,0:T(8,128)(2,1)S(1)}, bf16[128,2048]{1,0:T(8,128)(2,1)S(1)}, u32[]{:S(2)}, u32[]{:S(2)}) collective-permute-start(bf16[128,2048]{1,0:T(8,128)(2,1)S(1)} %collective-permute-done.4), channel_id=1, source_target_pairs={{0,2},{2,4},{4,6},{6,8},{8,10},{10,12},{12,14},{14,16},{16,18},{18... | collective-permute-start | bytes 1572872 | tf_op jit(solution)/shard_map/ppermute | solution.py:25
  85.4 12.5 %collective-permute-start.6 = (bf16[128,2048]{1,0:T(8,128)(2,1)S(1)}, bf16[128,2048]{1,0:T(8,128)(2,1)S(1)}, u32[]{:S(2)}, u32[]{:S(2)}) collective-permute-start(bf16[128,2048]{1,0:T(8,128)(2,1)S(1)} %collective-permute-done.5), channel_id=1, source_target_pairs={{0,2},{2,4},{4,6},{6,8},{8,10},{10,12},{12,14},{14,16},{16,18},{18... | collective-permute-start | bytes 1572872 | tf_op jit(solution)/shard_map/ppermute | solution.py:25
  97.8 14.2 %collective-permute-start.7 = (bf16[128,2048]{1,0:T(8,128)(2,1)S(1)}, bf16[128,2048]{1,0:T(8,128)(2,1)S(1)}, u32[]{:S(2)}, u32[]{:S(2)}) collective-permute-start(bf16[128,2048]{1,0:T(8,128)(2,1)S(1)} %collective-permute-done.6), channel_id=1, source_target_pairs={{0,2},{2,4},{4,6},{6,8},{8,10},{10,12},{12,14},{14,16},{16,18},{18... | collective-permute-start | bytes 1572872 | tf_op jit(solution)/shard_map/ppermute | solution.py:25
  108.8 24.2 %copy-start.7 = (bf16[128,2048]{1,0:T(8,128)(2,1)S(1)}, bf16[128,2048]{1,0:T(8,128)(2,1)}, u32[]{:S(2)}) copy-start(bf16[128,2048]{1,0:T(8,128)(2,1)} %copy-done.6) | copy-start | bytes 1572868
  112.0 15.3 %collective-permute-start.8 = (bf16[128,2048]{1,0:T(8,128)(2,1)S(1)}, bf16[128,2048]{1,0:T(8,128)(2,1)S(1)}, u32[]{:S(2)}, u32[]{:S(2)}) collective-permute-start(bf16[128,2048]{1,0:T(8,128)(2,1)S(1)} %collective-permute-done.7), channel_id=1, source_target_pairs={{0,2},{2,4},{4,6},{6,8},{8,10},{10,12},{12,14},{14,16},{16,18},{18... | collective-permute-start | bytes 1572872 | tf_op jit(solution)/shard_map/ppermute | solution.py:25
  127.3 16.5 %collective-permute-start.9 = (bf16[128,2048]{1,0:T(8,128)(2,1)S(1)}, bf16[128,2048]{1,0:T(8,128)(2,1)S(1)}, u32[]{:S(2)}, u32[]{:S(2)}) collective-permute-start(bf16[128,2048]{1,0:T(8,128)(2,1)S(1)} %collective-permute-done.8), channel_id=1, source_target_pairs={{0,2},{2,4},{4,6},{6,8},{8,10},{10,12},{12,14},{14,16},{16,18},{18... | collective-permute-start | bytes 1572872 | tf_op jit(solution)/shard_map/ppermute | solution.py:25
  143.8 16.3 %collective-permute-start.10 = (bf16[128,2048]{1,0:T(8,128)(2,1)S(1)}, bf16[128,2048]{1,0:T(8,128)(2,1)S(1)}, u32[]{:S(2)}, u32[]{:S(2)}) collective-permute-start(bf16[128,2048]{1,0:T(8,128)(2,1)S(1)} %collective-permute-done.9), channel_id=1, source_target_pairs={{0,2},{2,4},{4,6},{6,8},{8,10},{10,12},{12,14},{14,16},{16,18},{18... | collective-permute-start | bytes 1572872 | tf_op jit(solution)/shard_map/ppermute | solution.py:25
  160.1 17.4 %collective-permute-start.11 = (bf16[128,2048]{1,0:T(8,128)(2,1)S(1)}, bf16[128,2048]{1,0:T(8,128)(2,1)S(1)}, u32[]{:S(2)}, u32[]{:S(2)}) collective-permute-start(bf16[128,2048]{1,0:T(8,128)(2,1)S(1)} %collective-permute-done.10), channel_id=1, source_target_pairs={{0,2},{2,4},{4,6},{6,8},{8,10},{10,12},{12,14},{14,16},{16,18},{18... | collective-permute-start | bytes 1572872 | tf_op jit(solution)/shard_map/ppermute | solution.py:25
  177.5 18.3 %collective-permute-start.12 = (bf16[128,2048]{1,0:T(8,128)(2,1)S(1)}, bf16[128,2048]{1,0:T(8,128)(2,1)S(1)}, u32[]{:S(2)}, u32[]{:S(2)}) collective-permute-start(bf16[128,2048]{1,0:T(8,128)(2,1)S(1)} %collective-permute-done.11), channel_id=1, source_target_pairs={{0,2},{2,4},{4,6},{6,8},{8,10},{10,12},{12,14},{14,16},{16,18},{18... | collective-permute-start | bytes 1572872 | tf_op jit(solution)/shard_map/ppermute | solution.py:25
  195.8 16.4 %collective-permute-start.13 = (bf16[128,2048]{1,0:T(8,128)(2,1)S(1)}, bf16[128,2048]{1,0:T(8,128)(2,1)S(1)}, u32[]{:S(2)}, u32[]{:S(2)}) collective-permute-start(bf16[128,2048]{1,0:T(8,128)(2,1)S(1)} %collective-permute-done.12), channel_id=1, source_target_pairs={{0,2},{2,4},{4,6},{6,8},{8,10},{10,12},{12,14},{14,16},{16,18},{18... | collective-permute-start | bytes 1572872 | tf_op jit(solution)/shard_map/ppermute | solution.py:25
  212.2 12.8 %collective-permute-start.14 = (bf16[128,2048]{1,0:T(8,128)(2,1)S(1)}, bf16[128,2048]{1,0:T(8,128)(2,1)S(1)}, u32[]{:S(2)}, u32[]{:S(2)}) collective-permute-start(bf16[128,2048]{1,0:T(8,128)(2,1)S(1)} %collective-permute-done.13), channel_id=1, source_target_pairs={{0,2},{2,4},{4,6},{6,8},{8,10},{10,12},{12,14},{14,16},{16,18},{18... | collective-permute-start | bytes 1572872 | tf_op jit(solution)/shard_map/ppermute | solution.py:25
  227.1 22.3 %copy-start.10 = (f32[224,16]{0,1:T(8,128)S(1)}, f32[224,16]{0,1:T(8,128)}, u32[]{:S(2)}) copy-start(f32[224,16]{0,1:T(8,128)} %param.8) | copy-start | bytes 43012
  227.1 22.3 %copy-start.11 = (f32[224,16]{0,1:T(8,128)S(1)}, f32[224,16]{0,1:T(8,128)}, u32[]{:S(2)}) copy-start(f32[224,16]{0,1:T(8,128)} %param.10) | copy-start | bytes 43012
  228.3 83.7 %all-to-all-start.1 = ((bf16[128,16,224]{0,2,1:T(8,128)(2,1)}), bf16[128,16,224]{0,2,1:T(8,128)(2,1)S(1)}, u32[]{:S(2)}, u32[]{:S(2)}) async-start(bf16[128,16,224]{0,2,1:T(8,128)(2,1)} %bitcast.52), calls=%async_computation.1 | async-start | bytes 1835008 | tf_op jit(solution)/shard_map/all_to_all | solution.py:29
  249.1 131.6 %reduce-scatter.3.cloned.1.call-start = ((), (), s32[]{:S(2)}) async-start(), calls=%async_computation.5 | async-start | bytes 25165824 | tf_op jit(solution)/shard_map/reduce_scatter | solution.py:56
  354.4 220.4 %reduce-scatter.5.cloned.1.call-start = ((), (), s32[]{:S(2)}) async-start(), calls=%async_computation.6 | async-start | bytes 8912896 | tf_op jit(solution)/shard_map/reduce_scatter | solution.py:59
  383.0 41.2 %all-to-all-start = ((bf16[16,128,224]{1,2,0:T(8,128)(2,1)}), bf16[16,128,224]{1,2,0:T(8,128)(2,1)S(1)}, u32[]{:S(2)}, u32[]{:S(2)}) async-start(bf16[16,128,224]{1,2,0:T(8,128)(2,1)} %bitcast.117), calls=%async_computation | async-start | bytes 1835008 | tf_op jit(solution)/shard_map/all_to_all | solution.py:53
  (17 other events, 108.3 us)
Sparse Core Ops, SparseCore 0:
  226.0 42.9 all-gather.1
  354.5 26.1 reduce-scatter.2
  383.6 191.1 reduce-scatter.4
